TPU v7x, 512 devices: a whole 4x8x8 slice. The times are simulated.
512 devices in a mesh: layer: 2 (over core), row: 16 (over x, z_hi), col: 16 (over z_lo, y).
Axes of the slice: x: 4, y: 8, z: 8 (z_hi: 4, z_lo: 2; z = z_hi * 2 + z_lo), core: 2. Of those that a mesh axis runs over, the one named last changes fastest.
Arguments:
- rhs_sub: float32 [2, 3, 1, 16, 256, 512], P('layer', None, None, 'row', 'col'), may hold values from -6 to 6
- rhs_top: float32 [1, 16, 256, 512], P(None, 'row', 'col'), may hold values from -6 to 6
- lower_inv_sub: float32 [2, 3, 1, 16, 256, 256], P('layer', None, None, 'row', 'col'), as said below
- lower_inv_top: float32 [1, 16, 256, 256], P(None, 'row', 'col'), as said below
- upper_inv_sub: float32 [2, 3, 1, 16, 256, 256], P('layer', None, None, 'row', 'col'), as said below
- upper_inv_top: float32 [1, 16, 256, 256], P(None, 'row', 'col'), as said below
- lower_sub: float32 [2, 3, 1, 16, 1, 16, 256, 256], P('layer', None, None, 'row', None, 'col'), may hold values from -0.09375 to 0.09375
- lower_top: float32 [2, 3, 1, 16, 1, 16, 256, 256], P('layer', None, None, 'row', None, 'col'), may hold values from -0.0546875 to 0.0546875
- upper_sub: float32 [2, 3, 1, 16, 1, 16, 256, 256], P('layer', None, None, 'row', None, 'col'), may hold values from -0.0625 to 0.0625
- upper_top: float32 [2, 3, 1, 16, 1, 16, 256, 256], P('layer', None, None, 'row', None, 'col'), may hold values from -0.09375 to 0.09375
- block_pattern: int32 [2, 4, 3, 1, 16, 1, 16], P('layer', None, None, None, 'row', None, 'col'), may hold values 0 or 1
Outputs:
- solution_sub: float32 [2, 3, 1, 16, 256, 512], P('layer', None, None, 'row', 'col')
- solution_top: float32 [1, 16, 256, 512], P(None, 'row', 'col')
Inputs may be any that keep to these rules, and one draw needn't show every extreme that they name: `lower_inv_sub`: every 256 x 256 block is lower triangular with unit diagonal. `lower_inv_top`: every 256 x 256 block is lower triangular with unit diagonal. `upper_inv_sub`: every 256 x 256 block is upper triangular with unit diagonal. `upper_inv_top`: every 256 x 256 block is upper triangular with unit diagonal.
All inputs are finite; a program needn't handle non-finite values. No bound on the sum of `block_pattern` on one device may be relied on, other than what follows from the above.
Results may differ from a plain program's by a relative error of at most 0.00014.
Values sent between devices are 32-bit elements; how exact they have to be, the bound alone decides.
No kernel may reach another device: no remote copies, remote signals or barrier semaphores. Data moves between devices by JAX's collectives and lax.ppermute only.
A program may use at most 64 MiB of HBM per device.

v0:
```python
import jax
import jax.numpy as jnp
from jax import lax
from jax.sharding import PartitionSpec as P

HIGHEST = lax.Precision.HIGHEST


def broadcast(x, axis, root):
    mine = lax.axis_index(axis) == root
    return lax.psum(jnp.where(mine, x, jnp.zeros_like(x)), axis)


def couple(blocks, pattern, solution):
    weighted = solution[None] * pattern[:, :, None, None].astype(jnp.float32)
    return jnp.einsum("tsab,tsbn->tan", blocks, weighted, precision=HIGHEST)


def spread(whole_block):
    return broadcast(whole_block, "row", lax.axis_index("col"))


def on_device(
    rhs_sub,
    rhs_top,
    lower_inv_sub,
    lower_inv_top,
    upper_inv_sub,
    upper_inv_top,
    lower_sub,
    lower_top,
    upper_sub,
    upper_top,
    block_pattern,
):
    lower_list = [lower_inv_sub[0, level, :, 0] for level in range(3)] + [lower_inv_top[:, 0]]
    upper_list = [upper_inv_sub[0, level, :, 0] for level in range(3)] + [upper_inv_top[:, 0]]
    right_sides = [rhs_sub[0, level, :, 0] for level in range(3)] + [rhs_top[:, 0]]

    def solve(partial_value, right_side, inverse_rows, top):
        if partial_value is None:
            residual = right_side
        else:
            share = lax.psum_scatter(partial_value, "col", scatter_dimension=1, tiled=True)
            if top:
                share = lax.psum(share, "layer")
            residual = right_side - share
        return jnp.einsum(
            "kab,kbn->kan",
            inverse_rows,
            lax.all_gather(residual, "col", axis=1, tiled=True),
            precision=HIGHEST,
        )

    def copy_out(solution):
        return spread(lax.all_gather(solution, "col", axis=1, tiled=True))

    def blocks(array, pair):
        return array[0, pair, :, 0, :, 0]

    def pattern(kind, pair):
        return block_pattern[0, kind, pair, :, 0, :, 0]

    fore_zero = solve(None, right_sides[0], lower_list[0], False)
    copy_zero = copy_out(fore_zero)
    into_one = couple(blocks(lower_sub, 0), pattern(0, 0), copy_zero)
    into_two = couple(blocks(lower_sub, 1), pattern(0, 1), copy_zero)
    into_top = couple(blocks(lower_top, 0), pattern(1, 0), copy_zero)
    fore_one = solve(into_one, right_sides[1], lower_list[1], False)
    copy_one = copy_out(fore_one)
    into_two = into_two + couple(blocks(lower_sub, 2), pattern(0, 2), copy_one)
    into_top = into_top + couple(blocks(lower_top, 1), pattern(1, 1), copy_one)
    fore_two = solve(into_two, right_sides[2], lower_list[2], False)
    copy_two = copy_out(fore_two)
    into_top = into_top + couple(blocks(lower_top, 2), pattern(1, 2), copy_two)
    fore_top = solve(into_top, right_sides[3], lower_list[3], True)
    final_top = solve(None, fore_top, upper_list[3], False)
    down_top = copy_out(final_top)
    toward_two = couple(blocks(upper_top, 2), pattern(3, 2), down_top)
    toward_one = couple(blocks(upper_top, 1), pattern(3, 1), down_top)
    toward_zero = couple(blocks(upper_top, 0), pattern(3, 0), down_top)
    final_two = solve(toward_two, fore_two, upper_list[2], False)
    down_two = copy_out(final_two)
    toward_one = toward_one + couple(blocks(upper_sub, 2), pattern(2, 2), down_two)
    toward_zero = toward_zero + couple(blocks(upper_sub, 1), pattern(2, 1), down_two)
    final_one = solve(toward_one, fore_one, upper_list[1], False)
    down_one = copy_out(final_one)
    toward_zero = toward_zero + couple(blocks(upper_sub, 0), pattern(2, 0), down_one)
    final_zero = solve(toward_zero, fore_zero, upper_list[0], False)
    solution_sub = jnp.stack([final_zero, final_one, final_two])[None, :, :, None]
    solution_top = final_top[:, None]
    return (solution_sub, solution_top)


def solution(mesh):
    placed = (
        P("layer", None, None, "row", "col", None),
        P(None, "row", "col", None),
        P("layer", None, None, "row", "col", None),
        P(None, "row", "col", None),
        P("layer", None, None, "row", "col", None),
        P(None, "row", "col", None),
        P("layer", None, None, "row", None, "col", None, None),
        P("layer", None, None, "row", None, "col", None, None),
        P("layer", None, None, "row", None, "col", None, None),
        P("layer", None, None, "row", None, "col", None, None),
        P("layer", None, None, None, "row", None, "col"),
    )
    return jax.shard_map(
        on_device,
        mesh=mesh,
        in_specs=placed,
        out_specs=(P("layer", None, None, "row", "col", None), P(None, "row", "col", None)),
        check_vma=False,
    )
```

profile of v0, /device:TPU:2, one launch (start us, length us, event | category | flops | bytes accessed | tf_op | source)
XLA Modules:
  0.0 2184.0 jit_solution(2908091870607377560)
XLA Ops:
  8.0 37.7 %all-gather = f32[1,1,1,1,256,512]{5,4,3,2,1,0:T(8,128)S(1)} all-gather(f32[1,1,1,1,16,512]{5,4,3,2,1,0:T(8,128)S(1)} %get-tuple-element.8), channel_id=2, replica_groups=mesh['layer'=2,'row'=16,'col'=16] {'col'}, dimensions={4}, use_global_device_ids=true | all-gather | bytes 557056 | tf_op jit(solution)/shard_map/all_gather | solution.py:51
  46.1 32.3 %all-gather.1 = f32[256,512]{1,0:T(8,128)S(1)} all-gather(f32[16,512]{1,0:T(8,128)S(1)} %fusion.33), channel_id=3, replica_groups=mesh['layer'=2,'row'=16,'col'=16] {'col'}, dimensions={0}, use_global_device_ids=true | all-gather | bytes 557056 | tf_op jit(solution)/shard_map/all_gather | solution.py:56
  81.3 168.6 %all-reduce.13.cloned.1.call-done = f32[1,256,512]{2,1,0:T(8,128)} async-done(((f32[1,256,512]{2,1,0:T(8,128)}), f32[1,256,512]{2,1,0:T(8,128)}) %all-reduce.13.cloned.1.call-update) | async-done | bytes 524304 | tf_op jit(solution)/shard_map/psum | solution.py:11
  255.0 140.9 %all-reduce.25.cloned.1.call-done = f32[1,256,512]{2,0,1:T(1,128)} async-done(((f32[1,256,512]{2,0,1:T(1,128)}), f32[1,256,512]{2,0,1:T(1,128)}) %all-reduce.25.cloned.1.call-update) | async-done | bytes 524304
  396.7 35.3 %all_gather.44 = f32[1,256,512]{2,0,1:T(1,128)S(1)} all-gather(f32[1,16,512]{2,0,1:T(1,128)S(1)} %fusion.84), channel_id=1, replica_groups=mesh['layer'=2,'row'=16,'col'=16] {'col'}, dimensions={1}, use_global_device_ids=true | all-gather | bytes 557056 | tf_op jit(solution)/shard_map/all_gather | solution.py:51
  432.4 32.3 %all-gather.2 = f32[256,512]{1,0:T(8,128)S(1)} all-gather(f32[16,512]{1,0:T(8,128)S(1)} %bitcast.205), channel_id=4, replica_groups=mesh['layer'=2,'row'=16,'col'=16] {'col'}, dimensions={0}, use_global_device_ids=true | all-gather | bytes 557056 | tf_op jit(solution)/shard_map/all_gather | solution.py:56
  468.0 165.1 %all-reduce.15.cloned.1.call-done = f32[1,256,512]{2,1,0:T(8,128)} async-done(((f32[1,256,512]{2,1,0:T(8,128)}), f32[1,256,512]{2,1,0:T(8,128)}) %all-reduce.15.cloned.1.call-update) | async-done | bytes 524304 | tf_op jit(solution)/shard_map/psum | solution.py:11
  633.1 2.0 fusion.3
  638.1 141.0 %all-reduce.27.cloned.1.call-done = f32[1,256,512]{2,0,1:T(1,128)} async-done(((f32[1,256,512]{2,0,1:T(1,128)}), f32[1,256,512]{2,0,1:T(1,128)}) %all-reduce.27.cloned.1.call-update) | async-done | bytes 524304
  779.9 35.3 %all_gather.46 = f32[1,256,512]{2,0,1:T(1,128)S(1)} all-gather(f32[1,16,512]{2,0,1:T(1,128)S(1)} %fusion.83), channel_id=1, replica_groups=mesh['layer'=2,'row'=16,'col'=16] {'col'}, dimensions={1}, use_global_device_ids=true | all-gather | bytes 557056 | tf_op jit(solution)/shard_map/all_gather | solution.py:51
  815.6 32.3 %all-gather.3 = f32[256,512]{1,0:T(8,128)S(1)} all-gather(f32[16,512]{1,0:T(8,128)S(1)} %bitcast.206), channel_id=5, replica_groups=mesh['layer'=2,'row'=16,'col'=16] {'col'}, dimensions={0}, use_global_device_ids=true | all-gather | bytes 557056 | tf_op jit(solution)/shard_map/all_gather | solution.py:56
  851.3 165.0 %all-reduce.17.cloned.1.call-done = f32[1,256,512]{2,1,0:T(8,128)} async-done(((f32[1,256,512]{2,1,0:T(8,128)}), f32[1,256,512]{2,1,0:T(8,128)}) %all-reduce.17.cloned.1.call-update) | async-done | bytes 524304 | tf_op jit(solution)/shard_map/psum | solution.py:11
  1016.3 2.0 fusion.2
  1019.5 142.8 %all-reduce.29.cloned.1.call-done = f32[1,256,512]{2,0,1:T(1,128)} async-done(((f32[1,256,512]{2,0,1:T(1,128)}), f32[1,256,512]{2,0,1:T(1,128)}) %all-reduce.29.cloned.1.call-update) | async-done | bytes 524304
  1163.1 3.5 psum.52
  1166.7 35.3 %all_gather.48 = f32[1,256,512]{2,0,1:T(1,128)S(1)} all-gather(f32[1,16,512]{2,0,1:T(1,128)S(1)} %reshape_subtract_fusion), channel_id=1, replica_groups=mesh['layer'=2,'row'=16,'col'=16] {'col'}, dimensions={1}, use_global_device_ids=true | all-gather | bytes 557056 | tf_op jit(solution)/shard_map/all_gather | solution.py:51
  1202.3 32.8 %all-gather.4 = f32[256,512]{1,0:T(8,128)S(1)} all-gather(f32[16,512]{1,0:T(8,128)S(1)} %convolution_bitcast_fusion.3), channel_id=6, replica_groups=mesh['layer'=2,'row'=16,'col'=16] {'col'}, dimensions={0}, use_global_device_ids=true | all-gather | bytes 557056 | tf_op jit(solution)/shard_map/all_gather | solution.py:51
  1235.5 34.6 %all-gather.5 = f32[256,512]{1,0:T(8,128)S(1)} all-gather(f32[16,512]{1,0:T(8,128)S(1)} %bitcast.211), channel_id=7, replica_groups=mesh['layer'=2,'row'=16,'col'=16] {'col'}, dimensions={0}, use_global_device_ids=true | all-gather | bytes 557056 | tf_op jit(solution)/shard_map/all_gather | solution.py:56
  1271.6 165.4 %all-reduce.19.cloned.1.call-done = f32[1,256,512]{2,1,0:T(8,128)} async-done(((f32[1,256,512]{2,1,0:T(8,128)}), f32[1,256,512]{2,1,0:T(8,128)}) %all-reduce.19.cloned.1.call-update) | async-done | bytes 524304 | tf_op jit(solution)/shard_map/psum | solution.py:11
  1437.0 2.5 convolution_bitcast_fusion
  1439.5 75.0 %reduce-scatter.4.cloned.1.call-done = f32[1,16,512]{2,1,0:T(8,128)} async-done(((f32[1,256,512]{2,1,0:T(8,128)}), f32[1,16,512]{2,1,0:T(8,128)}) %reduce-scatter.4.cloned.1.call-update) | async-done | bytes 32784 | tf_op jit(solution)/shard_map/reduce_scatter | solution.py:44
  1515.3 33.9 %all_gather.51 = f32[1,256,512]{2,1,0:T(8,128)S(1)} all-gather(f32[1,16,512]{2,1,0:T(8,128)S(1)} %bitcast_subtract_fusion.1), channel_id=1, replica_groups=mesh['layer'=2,'row'=16,'col'=16] {'col'}, dimensions={1}, use_global_device_ids=true | all-gather | bytes 557056 | tf_op jit(solution)/shard_map/all_gather | solution.py:51
  1549.6 33.3 %all-gather.6 = f32[256,512]{1,0:T(8,128)S(1)} all-gather(f32[16,512]{1,0:T(8,128)S(1)} %bitcast.207), channel_id=8, replica_groups=mesh['layer'=2,'row'=16,'col'=16] {'col'}, dimensions={0}, use_global_device_ids=true | all-gather | bytes 557056 | tf_op jit(solution)/shard_map/all_gather | solution.py:56
  1586.2 164.1 %all-reduce.21.cloned.1.call-done = f32[1,256,512]{2,1,0:T(8,128)} async-done(((f32[1,256,512]{2,1,0:T(8,128)}), f32[1,256,512]{2,1,0:T(8,128)}) %all-reduce.21.cloned.1.call-update) | async-done | bytes 524304 | tf_op jit(solution)/shard_map/psum | solution.py:11
  1750.4 2.5 fusion.1
  1754.8 73.1 %reduce-scatter.6.cloned.1.call-done = f32[1,16,512]{2,1,0:T(8,128)} async-done(((f32[1,256,512]{2,1,0:T(8,128)}), f32[1,16,512]{2,1,0:T(8,128)}) %reduce-scatter.6.cloned.1.call-update) | async-done | bytes 32784 | tf_op jit(solution)/shard_map/reduce_scatter | solution.py:44
  1828.6 33.8 %all_gather.53 = f32[1,256,512]{2,1,0:T(8,128)S(1)} all-gather(f32[1,16,512]{2,1,0:T(8,128)S(1)} %bitcast_subtract_fusion), channel_id=1, replica_groups=mesh['layer'=2,'row'=16,'col'=16] {'col'}, dimensions={1}, use_global_device_ids=true | all-gather | bytes 557056 | tf_op jit(solution)/shard_map/all_gather | solution.py:51
  1862.8 33.3 %all-gather.7 = f32[256,512]{1,0:T(8,128)S(1)} all-gather(f32[16,512]{1,0:T(8,128)S(1)} %bitcast.209), channel_id=9, replica_groups=mesh['layer'=2,'row'=16,'col'=16] {'col'}, dimensions={0}, use_global_device_ids=true | all-gather | bytes 557056 | tf_op jit(solution)/shard_map/all_gather | solution.py:56
  1898.8 165.3 %all-reduce.23.cloned.1.call-done = f32[1,256,512]{2,1,0:T(8,128)} async-done(((f32[1,256,512]{2,1,0:T(8,128)}), f32[1,256,512]{2,1,0:T(8,128)}) %all-reduce.23.cloned.1.call-update) | async-done | bytes 524304 | tf_op jit(solution)/shard_map/psum | solution.py:11
  2064.1 2.5 fusion
  2066.6 75.0 %reduce-scatter.8.cloned.1.call-done = f32[1,16,512]{2,1,0:T(8,128)} async-done(((f32[1,256,512]{2,1,0:T(8,128)}), f32[1,16,512]{2,1,0:T(8,128)}) %reduce-scatter.8.cloned.1.call-update) | async-done | bytes 32784 | tf_op jit(solution)/shard_map/reduce_scatter | solution.py:44
  2142.4 33.8 %all_gather.55 = f32[1,256,512]{2,1,0:T(8,128)S(1)} all-gather(f32[1,16,512]{2,1,0:T(8,128)S(1)} %bitcast_subtract_fusion.2), channel_id=1, replica_groups=mesh['layer'=2,'row'=16,'col'=16] {'col'}, dimensions={1}, use_global_device_ids=true | all-gather | bytes 557056 | tf_op jit(solution)/shard_map/all_gather | solution.py:51
  (89 shorter events, 28.9 us)
Async XLA Ops:
  7.2 1194.8 %copy-start = (f32[1,1,16,256]{3,2,1,0:T(8,128)S(1)}, f32[1,1,16,256]{3,2,1,0:T(8,128)}, u32[]{:S(2)}) copy-start(f32[1,1,16,256]{3,2,1,0:T(8,128)} %param.14) | copy-start | bytes 49156
  7.2 242.7 %all-reduce.13.cloned.1.call-start = ((), (), s32[]{:S(2)}) async-start(), calls=%async_computation.3 | async-start | bytes 1048576 | tf_op jit(solution)/shard_map/psum | solution.py:11
  8.0 37.7 %copy-start.10 = (f32[1,3,1,1,16,256]{5,4,3,2,1,0:T(8,128)S(1)}, f32[1,3,1,1,16,256]{5,4,3,2,1,0:T(8,128)}, u32[]{:S(2)}) copy-start(f32[1,3,1,1,16,256]{5,4,3,2,1,0:T(8,128)} %param.13) | copy-start | bytes 147460
  78.4 171.5 %copy-start.6 = (f32[1,3,1,1,1,1,256,256]{7,6,5,4,3,2,1,0:T(8,128)S(1)}, f32[1,3,1,1,1,1,256,256]{7,6,5,4,3,2,1,0:T(8,128)}, u32[]{:S(2)}) copy-start(f32[1,3,1,1,1,1,256,256]{7,6,5,4,3,2,1,0:T(8,128)} %param.17) | copy-start | bytes 2359300
  79.3 0.7 copy-start.13
  79.3 316.6 %all-reduce.25.cloned.1.call-start = ((), (), s32[]{:S(2)}) async-start(), calls=%async_computation.12 | async-start | bytes 1048576
  253.0 380.1 %all-reduce.15.cloned.1.call-start = ((), (), s32[]{:S(2)}) async-start(), calls=%async_computation.4 | async-start | bytes 1048576 | tf_op jit(solution)/shard_map/psum | solution.py:11
  465.6 1.4 copy-start.1
  465.6 313.5 %all-reduce.27.cloned.1.call-start = ((), (), s32[]{:S(2)}) async-start(), calls=%async_computation.13 | async-start | bytes 1048576
  636.2 380.1 %all-reduce.17.cloned.1.call-start = ((), (), s32[]{:S(2)}) async-start(), calls=%async_computation.5 | async-start | bytes 1048576 | tf_op jit(solution)/shard_map/psum | solution.py:11
  847.9 1.3 copy-start.7
  848.8 313.5 %all-reduce.29.cloned.1.call-start = ((), (), s32[]{:S(2)}) async-start(), calls=%async_computation.14 | async-start | bytes 1048576
  849.3 1.0 copy-start.3
  1019.4 417.5 %all-reduce.19.cloned.1.call-start = ((), (), s32[]{:S(2)}) async-start(), calls=%async_computation.6 | async-start | bytes 1048576 | tf_op jit(solution)/shard_map/psum | solution.py:11
  1163.1 3.5 copy-start.12
  1202.3 32.8 %copy-start.14 = (f32[1,1,16,256]{3,2,1,0:T(8,128)S(1)}, f32[1,1,16,256]{3,2,1,0:T(8,128)}, u32[]{:S(2)}) copy-start(f32[1,1,16,256]{3,2,1,0:T(8,128)} %param.16) | copy-start | bytes 49156
  1235.5 34.6 %copy-start.9 = (f32[512,16]{0,1:T(8,128)}, f32[512,16]{0,1:T(8,128)S(1)}, u32[]{:S(2)}) copy-start(f32[512,16]{0,1:T(8,128)S(1)} %fusion.88) | copy-start | bytes 98308
  1270.0 166.9 %copy-start.5 = (f32[1,3,1,1,1,1,256,256]{7,6,5,4,3,2,1,0:T(8,128)S(1)}, f32[1,3,1,1,1,1,256,256]{7,6,5,4,3,2,1,0:T(8,128)}, u32[]{:S(2)}) copy-start(f32[1,3,1,1,1,1,256,256]{7,6,5,4,3,2,1,0:T(8,128)} %param.20) | copy-start | bytes 2359300
  1270.9 243.7 %reduce-scatter.4.cloned.1.call-start = ((), (), s32[]{:S(2)}) async-start(), calls=%async_computation.7 | async-start | bytes 557056 | tf_op jit(solution)/shard_map/reduce_scatter | solution.py:44
  1439.5 310.9 %all-reduce.21.cloned.1.call-start = ((), (), s32[]{:S(2)}) async-start(), calls=%async_computation.8 | async-start | bytes 1048576 | tf_op jit(solution)/shard_map/psum | solution.py:11
  1515.3 33.9 %copy-start.11 = (f32[1,3,1,1,16,256]{5,4,3,2,1,0:T(8,128)S(1)}, f32[1,3,1,1,16,256]{5,4,3,2,1,0:T(8,128)}, u32[]{:S(2)}) copy-start(f32[1,3,1,1,16,256]{5,4,3,2,1,0:T(8,128)} %param.15) | copy-start | bytes 147460
  1583.8 1.8 copy-start.2
  1583.8 166.6 %copy-start.8 = (f32[1,3,1,1,1,1,256,256]{7,6,5,4,3,2,1,0:T(8,128)S(1)}, f32[1,3,1,1,1,1,256,256]{7,6,5,4,3,2,1,0:T(8,128)}, u32[]{:S(2)}) copy-start(f32[1,3,1,1,1,1,256,256]{7,6,5,4,3,2,1,0:T(8,128)} %param.19) | copy-start | bytes 2359300
  1583.8 244.0 %reduce-scatter.6.cloned.1.call-start = ((), (), s32[]{:S(2)}) async-start(), calls=%async_computation.9 | async-start | bytes 557056 | tf_op jit(solution)/shard_map/reduce_scatter | solution.py:44
  1752.9 311.2 %all-reduce.23.cloned.1.call-start = ((), (), s32[]{:S(2)}) async-start(), calls=%async_computation.10 | async-start | bytes 1048576 | tf_op jit(solution)/shard_map/psum | solution.py:11
  1897.0 244.6 %reduce-scatter.8.cloned.1.call-start = ((), (), s32[]{:S(2)}) async-start(), calls=%async_computation.11 | async-start | bytes 557056 | tf_op jit(solution)/shard_map/reduce_scatter | solution.py:44
  1897.1 1.0 copy-start.4
Sparse Core Ops, SparseCore 0:
  79.4 170.4 all-reduce.12
  253.1 142.7 all-reduce.24
  465.8 167.2 all-reduce.14
  636.3 142.7 all-reduce.26
  849.0 167.2 all-reduce.16
  1019.6 142.7 all-reduce.28
  1271.0 165.8 all-reduce.18
  1439.7 74.7 reduce-scatter.3
  1583.9 166.4 all-reduce.20
  1753.0 74.7 reduce-scatter.5
  1897.1 166.9 all-reduce.22
  2066.8 74.7 reduce-scatter.7
where the time goes:
time: 2190 us; the launch traced here: 2180 us
  waiting for transfers between devices  1640 us (75%)
  blocking collectives  479 us (22%)
  between operations  22.8 us (1%)
    psum x6, waiting for transfers between devices, broadcast(): return lax.psum(jnp.where(mine, x, jnp.zeros_like(x)), axis)  994 us
    unnamed x15, waiting for transfers between devices  425 us
    all_gather x8, blocking collectives, solve(): lax.all_gather(residual, 'col', axis=1, tiled=True)  278 us
    reduce_scatter x3, waiting for transfers between devices, solve(): lax.psum_scatter(partial_value, 'col', scatter_dimension=1, tiled=True)  223 us
    all_gather x6, blocking collectives, copy_out(): return spread(lax.all_gather(solution, 'col', axis=1, tiled=True))  198 us
  transfers between devices with their start and end apart: 12, of which 12 were waited for; matrix products, arithmetic and copies ran while one was open for 0% of the time, Pallas kernels for 0%

commit v1 on v0

--- a/solution.py
+++ b/solution.py
@@ -53,7 +53,11 @@
         )
 
     def copy_out(solution):
-        return spread(lax.all_gather(solution, "col", axis=1, tiled=True))
+        return spread(
+            jnp.concatenate(
+                lax.all_to_all(jnp.stack([solution] * lax.axis_size("col")), "col", 0, 0), axis=1
+            )
+        )
 
     def blocks(array, pair):
         return array[0, pair, :, 0, :, 0]

time: 2190 us -> 2090 us (0.954)
  blocking collectives: 479 us -> 332 us
  waiting for transfers between devices: 1640 us -> 1680 us
    all_gather x6 -> x0, blocking collectives: 198 us -> none  [copy_out(): return spread(lax.all_gather(solution, 'col', axis=1, tiled=True))]
    all_to_all x0 -> x3, blocking collectives: none -> 42.7 us  [copy_out(): lax.all_to_all(jnp.stack([solution] * lax.axis_size('col')), 'col', 0, 0)]
    all_to_all x0 -> x3, waiting for transfers between devices: none -> 30.3 us  [copy_out(): lax.all_to_all(jnp.stack([solution] * lax.axis_size('col')), 'col', 0, 0)]
  transfers between devices with their start and end apart: 12 -> 15, of which waited for: 12 -> 15; matrix products, arithmetic and copies ran while one was open for 0% -> 0% of each run, Pallas kernels for 0% -> 0%
where the time goes in v1:
time: 2090 us
  waiting for transfers between devices  1680 us (80%)
  blocking collectives  332 us (16%)
  between operations  22.7 us (1%)
  matrix products  21.7 us (1%)
    psum x6, waiting for transfers between devices, broadcast(): return lax.psum(jnp.where(mine, x, jnp.zeros_like(x)), axis)  1000 us
    unnamed x15, waiting for transfers between devices  427 us
    all_gather x8, blocking collectives, solve(): lax.all_gather(residual, 'col', axis=1, tiled=True)  285 us
    reduce_scatter x3, waiting for transfers between devices, solve(): lax.psum_scatter(partial_value, 'col', scatter_dimension=1, tiled=True)  225 us
    all_to_all x3, blocking collectives, copy_out(): lax.all_to_all(jnp.stack([solution] * lax.axis_size('col')), 'col', 0, 0)  42.7 us
  transfers between devices with their start and end apart: 15, of which 15 were waited for; matrix products, arithmetic and copies ran while one was open for 0% of the time, Pallas kernels for 0%

profile of v1, /device:TPU:2, one launch (start us, length us, event | category | flops | bytes accessed | tf_op | source)
XLA Modules:
  0.0 2092.9 jit_solution(14755541993947713519)
XLA Ops:
  8.0 37.7 %all-gather = f32[1,1,1,1,256,512]{5,4,3,2,1,0:T(8,128)S(1)} all-gather(f32[1,1,1,1,16,512]{5,4,3,2,1,0:T(8,128)S(1)} %get-tuple-element.8), channel_id=2, replica_groups=mesh['layer'=2,'row'=16,'col'=16] {'col'}, dimensions={4}, use_global_device_ids=true | all-gather | bytes 557056 | tf_op jit(solution)/shard_map/all_gather | solution.py:51
  46.9 3.6 all-to-all-start
  50.6 11.3 all-to-all-done
  64.7 169.1 %all-reduce.13.cloned.1.call-done = f32[1,256,512]{2,1,0:T(8,128)} async-done(((f32[1,256,512]{2,1,0:T(8,128)}), f32[1,256,512]{2,1,0:T(8,128)}) %all-reduce.13.cloned.1.call-update) | async-done | bytes 524304 | tf_op jit(solution)/shard_map/psum | solution.py:11
  239.0 140.8 %all-reduce.25.cloned.1.call-done = f32[1,256,512]{2,0,1:T(1,128)} async-done(((f32[1,256,512]{2,0,1:T(1,128)}), f32[1,256,512]{2,0,1:T(1,128)}) %all-reduce.25.cloned.1.call-update) | async-done | bytes 524304
  380.6 37.5 %all_gather.25 = f32[1,256,512]{2,0,1:T(1,128)S(1)} all-gather(f32[1,16,512]{2,0,1:T(1,128)S(1)} %fusion.84), channel_id=1, replica_groups=mesh['layer'=2,'row'=16,'col'=16] {'col'}, dimensions={1}, use_global_device_ids=true | all-gather | bytes 557056 | tf_op jit(solution)/shard_map/all_gather | solution.py:51
  418.6 14.0 all_to_all.30
  435.8 165.8 %all-reduce.15.cloned.1.call-done = f32[1,256,512]{2,1,0:T(8,128)} async-done(((f32[1,256,512]{2,1,0:T(8,128)}), f32[1,256,512]{2,1,0:T(8,128)}) %all-reduce.15.cloned.1.call-update) | async-done | bytes 524304 | tf_op jit(solution)/shard_map/psum | solution.py:11
  604.8 142.9 %all-reduce.27.cloned.1.call-done = f32[1,256,512]{2,0,1:T(1,128)} async-done(((f32[1,256,512]{2,0,1:T(1,128)}), f32[1,256,512]{2,0,1:T(1,128)}) %all-reduce.27.cloned.1.call-update) | async-done | bytes 524304
  748.5 35.7 %all_gather.26 = f32[1,256,512]{2,0,1:T(1,128)S(1)} all-gather(f32[1,16,512]{2,0,1:T(1,128)S(1)} %fusion.83), channel_id=1, replica_groups=mesh['layer'=2,'row'=16,'col'=16] {'col'}, dimensions={1}, use_global_device_ids=true | all-gather | bytes 557056 | tf_op jit(solution)/shard_map/all_gather | solution.py:51
  785.4 3.6 all-to-all-start.2
  791.0 9.4 all-to-all-done.2
  803.4 166.4 %all-reduce.17.cloned.1.call-done = f32[1,256,512]{2,1,0:T(8,128)} async-done(((f32[1,256,512]{2,1,0:T(8,128)}), f32[1,256,512]{2,1,0:T(8,128)}) %all-reduce.17.cloned.1.call-update) | async-done | bytes 524304 | tf_op jit(solution)/shard_map/psum | solution.py:11
  972.9 142.8 %all-reduce.29.cloned.1.call-done = f32[1,256,512]{2,0,1:T(1,128)} async-done(((f32[1,256,512]{2,0,1:T(1,128)}), f32[1,256,512]{2,0,1:T(1,128)}) %all-reduce.29.cloned.1.call-update) | async-done | bytes 524304
  1116.5 3.5 psum.52
  1120.1 35.3 %all_gather.27 = f32[1,256,512]{2,0,1:T(1,128)S(1)} all-gather(f32[1,16,512]{2,0,1:T(1,128)S(1)} %reshape_subtract_fusion), channel_id=1, replica_groups=mesh['layer'=2,'row'=16,'col'=16] {'col'}, dimensions={1}, use_global_device_ids=true | all-gather | bytes 557056 | tf_op jit(solution)/shard_map/all_gather | solution.py:51
  1155.8 34.6 %all-gather.1 = f32[256,512]{1,0:T(8,128)S(1)} all-gather(f32[16,512]{1,0:T(8,128)S(1)} %convolution_bitcast_fusion.3), channel_id=3, replica_groups=mesh['layer'=2,'row'=16,'col'=16] {'col'}, dimensions={0}, use_global_device_ids=true | all-gather | bytes 557056 | tf_op jit(solution)/shard_map/all_gather | solution.py:51
  1191.4 14.6 all_to_all.31
  1207.5 168.1 %all-reduce.19.cloned.1.call-done = f32[1,256,512]{2,1,0:T(8,128)} async-done(((f32[1,256,512]{2,1,0:T(8,128)}), f32[1,256,512]{2,1,0:T(8,128)}) %all-reduce.19.cloned.1.call-update) | async-done | bytes 524304 | tf_op jit(solution)/shard_map/psum | solution.py:11
  1378.2 75.0 %reduce-scatter.4.cloned.1.call-done = f32[1,16,512]{2,1,0:T(8,128)} async-done(((f32[1,256,512]{2,1,0:T(8,128)}), f32[1,16,512]{2,1,0:T(8,128)}) %reduce-scatter.4.cloned.1.call-update) | async-done | bytes 32784 | tf_op jit(solution)/shard_map/reduce_scatter | solution.py:44
  1454.0 35.9 %all_gather.29 = f32[1,256,512]{2,1,0:T(8,128)S(1)} all-gather(f32[1,16,512]{2,1,0:T(8,128)S(1)} %bitcast_subtract_fusion.1), channel_id=1, replica_groups=mesh['layer'=2,'row'=16,'col'=16] {'col'}, dimensions={1}, use_global_device_ids=true | all-gather | bytes 557056 | tf_op jit(solution)/shard_map/all_gather | solution.py:51
  1490.4 14.0 all_to_all.32
  1507.4 166.2 %all-reduce.21.cloned.1.call-done = f32[1,256,512]{2,1,0:T(8,128)} async-done(((f32[1,256,512]{2,1,0:T(8,128)}), f32[1,256,512]{2,1,0:T(8,128)}) %all-reduce.21.cloned.1.call-update) | async-done | bytes 524304 | tf_op jit(solution)/shard_map/psum | solution.py:11
  1673.6 2.5 fusion.1
  1676.1 74.9 %reduce-scatter.6.cloned.1.call-done = f32[1,16,512]{2,1,0:T(8,128)} async-done(((f32[1,256,512]{2,1,0:T(8,128)}), f32[1,16,512]{2,1,0:T(8,128)}) %reduce-scatter.6.cloned.1.call-update) | async-done | bytes 32784 | tf_op jit(solution)/shard_map/reduce_scatter | solution.py:44
  1751.8 34.9 %all_gather.30 = f32[1,256,512]{2,1,0:T(8,128)S(1)} all-gather(f32[1,16,512]{2,1,0:T(8,128)S(1)} %bitcast_subtract_fusion), channel_id=1, replica_groups=mesh['layer'=2,'row'=16,'col'=16] {'col'}, dimensions={1}, use_global_device_ids=true | all-gather | bytes 557056 | tf_op jit(solution)/shard_map/all_gather | solution.py:51
  1788.0 3.6 all-to-all-start.5
  1793.4 9.5 all-to-all-done.5
  1805.6 167.4 %all-reduce.23.cloned.1.call-done = f32[1,256,512]{2,1,0:T(8,128)} async-done(((f32[1,256,512]{2,1,0:T(8,128)}), f32[1,256,512]{2,1,0:T(8,128)}) %all-reduce.23.cloned.1.call-update) | async-done | bytes 524304 | tf_op jit(solution)/shard_map/psum | solution.py:11
  1973.0 2.5 fusion
  1975.5 75.0 %reduce-scatter.8.cloned.1.call-done = f32[1,16,512]{2,1,0:T(8,128)} async-done(((f32[1,256,512]{2,1,0:T(8,128)}), f32[1,16,512]{2,1,0:T(8,128)}) %reduce-scatter.8.cloned.1.call-update) | async-done | bytes 32784 | tf_op jit(solution)/shard_map/reduce_scatter | solution.py:44
  2051.2 33.8 %all_gather.31 = f32[1,256,512]{2,1,0:T(8,128)S(1)} all-gather(f32[1,16,512]{2,1,0:T(8,128)S(1)} %bitcast_subtract_fusion.2), channel_id=1, replica_groups=mesh['layer'=2,'row'=16,'col'=16] {'col'}, dimensions={1}, use_global_device_ids=true | all-gather | bytes 557056 | tf_op jit(solution)/shard_map/all_gather | solution.py:51
  (98 shorter events, 38.2 us)
Async XLA Ops:
  7.2 1148.2 %copy-start = (f32[1,1,16,256]{3,2,1,0:T(8,128)S(1)}, f32[1,1,16,256]{3,2,1,0:T(8,128)}, u32[]{:S(2)}) copy-start(f32[1,1,16,256]{3,2,1,0:T(8,128)} %param.14) | copy-start | bytes 49156
  8.0 37.7 %copy-start.10 = (f32[1,3,1,1,16,256]{5,4,3,2,1,0:T(8,128)S(1)}, f32[1,3,1,1,16,256]{5,4,3,2,1,0:T(8,128)}, u32[]{:S(2)}) copy-start(f32[1,3,1,1,16,256]{5,4,3,2,1,0:T(8,128)} %param.13) | copy-start | bytes 147460
  46.9 15.0 all-to-all-start
  50.5 183.3 %all-reduce.13.cloned.1.call-start = ((), (), s32[]{:S(2)}) async-start(), calls=%async_computation.9 | async-start | bytes 1048576 | tf_op jit(solution)/shard_map/psum | solution.py:11
  50.6 183.3 %copy-start.6 = (f32[1,3,1,1,1,1,256,256]{7,6,5,4,3,2,1,0:T(8,128)S(1)}, f32[1,3,1,1,1,1,256,256]{7,6,5,4,3,2,1,0:T(8,128)}, u32[]{:S(2)}) copy-start(f32[1,3,1,1,1,1,256,256]{7,6,5,4,3,2,1,0:T(8,128)} %param.17) | copy-start | bytes 2359300
  62.7 0.7 copy-start.13
  62.7 317.1 %all-reduce.25.cloned.1.call-start = ((), (), s32[]{:S(2)}) async-start(), calls=%async_computation.18 | async-start | bytes 1048576
  236.9 364.7 %all-reduce.15.cloned.1.call-start = ((), (), s32[]{:S(2)}) async-start(), calls=%async_computation.10 | async-start | bytes 1048576 | tf_op jit(solution)/shard_map/psum | solution.py:11
  433.5 1.3 copy-start.1
  433.5 314.1 %all-reduce.27.cloned.1.call-start = ((), (), s32[]{:S(2)}) async-start(), calls=%async_computation.19 | async-start | bytes 1048576
  785.4 15.0 all-to-all-start.2
  789.0 180.7 %all-reduce.17.cloned.1.call-start = ((), (), s32[]{:S(2)}) async-start(), calls=%async_computation.11 | async-start | bytes 1048576 | tf_op jit(solution)/shard_map/psum | solution.py:11
  791.0 10.4 copy-start.7
  801.3 314.5 %all-reduce.29.cloned.1.call-start = ((), (), s32[]{:S(2)}) async-start(), calls=%async_computation.20 | async-start | bytes 1048576
  801.3 1.0 copy-start.3
  972.9 402.7 %all-reduce.19.cloned.1.call-start = ((), (), s32[]{:S(2)}) async-start(), calls=%async_computation.12 | async-start | bytes 1048576 | tf_op jit(solution)/shard_map/psum | solution.py:11
  1116.5 3.5 copy-start.12
  1155.8 34.6 %copy-start.14 = (f32[1,1,16,256]{3,2,1,0:T(8,128)S(1)}, f32[1,1,16,256]{3,2,1,0:T(8,128)}, u32[]{:S(2)}) copy-start(f32[1,1,16,256]{3,2,1,0:T(8,128)} %param.16) | copy-start | bytes 49156
  1190.7 0.6 copy-start.9
  1206.0 169.6 %copy-start.5 = (f32[1,3,1,1,1,1,256,256]{7,6,5,4,3,2,1,0:T(8,128)S(1)}, f32[1,3,1,1,1,1,256,256]{7,6,5,4,3,2,1,0:T(8,128)}, u32[]{:S(2)}) copy-start(f32[1,3,1,1,1,1,256,256]{7,6,5,4,3,2,1,0:T(8,128)} %param.20) | copy-start | bytes 2359300
  1206.9 246.4 %reduce-scatter.4.cloned.1.call-start = ((), (), s32[]{:S(2)}) async-start(), calls=%async_computation.13 | async-start | bytes 557056 | tf_op jit(solution)/shard_map/reduce_scatter | solution.py:44
  1378.1 295.5 %all-reduce.21.cloned.1.call-start = ((), (), s32[]{:S(2)}) async-start(), calls=%async_computation.14 | async-start | bytes 1048576 | tf_op jit(solution)/shard_map/psum | solution.py:11
  1454.0 35.9 %copy-start.11 = (f32[1,3,1,1,16,256]{5,4,3,2,1,0:T(8,128)S(1)}, f32[1,3,1,1,16,256]{5,4,3,2,1,0:T(8,128)}, u32[]{:S(2)}) copy-start(f32[1,3,1,1,16,256]{5,4,3,2,1,0:T(8,128)} %param.15) | copy-start | bytes 147460
  1505.3 1.4 copy-start.2
  1505.3 168.3 %copy-start.8 = (f32[1,3,1,1,1,1,256,256]{7,6,5,4,3,2,1,0:T(8,128)S(1)}, f32[1,3,1,1,1,1,256,256]{7,6,5,4,3,2,1,0:T(8,128)}, u32[]{:S(2)}) copy-start(f32[1,3,1,1,1,1,256,256]{7,6,5,4,3,2,1,0:T(8,128)} %param.19) | copy-start | bytes 2359300
  1505.3 245.8 %reduce-scatter.6.cloned.1.call-start = ((), (), s32[]{:S(2)}) async-start(), calls=%async_computation.15 | async-start | bytes 557056 | tf_op jit(solution)/shard_map/reduce_scatter | solution.py:44
  1788.0 15.0 all-to-all-start.5
  1791.6 181.4 %all-reduce.23.cloned.1.call-start = ((), (), s32[]{:S(2)}) async-start(), calls=%async_computation.16 | async-start | bytes 1048576 | tf_op jit(solution)/shard_map/psum | solution.py:11
  1803.8 246.6 %reduce-scatter.8.cloned.1.call-start = ((), (), s32[]{:S(2)}) async-start(), calls=%async_computation.17 | async-start | bytes 557056 | tf_op jit(solution)/shard_map/reduce_scatter | solution.py:44
  1803.9 1.0 copy-start.4
Sparse Core Ops, SparseCore 0:
  62.9 170.9 all-reduce.12
  237.0 142.7 all-reduce.24
  433.6 167.9 all-reduce.14
  604.9 142.7 all-reduce.26
  801.4 168.3 all-reduce.16
  973.0 142.7 all-reduce.28
  1207.0 168.5 all-reduce.18
  1378.4 74.7 reduce-scatter.3
  1505.4 168.1 all-reduce.20
  1676.2 74.7 reduce-scatter.5
  1804.0 169.0 all-reduce.22
  1975.7 74.7 reduce-scatter.7
